TPU v7x, 512 devices: a whole 4x8x8 slice. The times are simulated.
512 devices in a mesh: snode: 64 (over z, y), rows: 8 (over x, core).
Axes of the slice: x: 4, y: 8, z: 8, core: 2. Of those that a mesh axis runs over, the one named last changes fastest.
Arguments:
- anc_store: bfloat16 [8192, 8192], P('snode'), may hold values from -9 to 9
- patterns: int32 [64, 8], replicated, may hold values from 0 to 63, all different within a row
- tile_counts: int32 [64], replicated, may hold values from 1 to 8, 448 in all
- tile_owner: int32 [64], replicated, may hold values from 0 to 63, as said below
- l_offdiag: bfloat16 [65536, 512], P(('snode', 'rows')), may hold values from -0.25 to 0.25
- diag_inverse: bfloat16 [32768, 512], P(('snode', 'rows')), may hold values from -1 to 2, as said below
Outputs:
- sigma_offdiag: bfloat16 [65536, 512], P(('snode', 'rows'))
- sigma_diag: float32 [32768, 512], P(('snode', 'rows'))
Inputs may be any that keep to these rules, and one draw needn't show every extreme that they name: `patterns`: each supernode's row names 8 different ancestor tiles. Slots before tile_counts[s] of a supernode's pattern are live, the rest padding; some supernode has all 8 slots live. `tile_owner`: a permutation of the ancestor tiles. `diag_inverse`: each supernode's block of 512 rows is lower triangular with diagonal entries between 1 and 2.
All inputs are finite; a program needn't handle non-finite values.
Results may differ from a plain program's by a relative error of at most 0.014.
Values may be sent and summed in bfloat16 or wider, within the bound.
A program may use at most 64 MiB of HBM per device.

v0:
```python
import jax
import jax.numpy as jnp
from jax import lax
from jax.sharding import PartitionSpec as P


def row_block(matrix, index):
    return lax.dynamic_index_in_dim(matrix, index, 0, keepdims=False)


def per_device(anc_store, patterns, tile_counts, tile_owner, l_offdiag, diag_inverse):
    tile_rows = anc_store.shape[0]
    pool_size = tile_owner.shape[0]
    group_count = patterns.shape[0]
    pattern_len = patterns.shape[1]
    group_id = lax.axis_index("snode")
    part_id = lax.axis_index("rows")
    local_tiles = l_offdiag.shape[0] // tile_rows
    band_rows = diag_inverse.shape[0]
    band_start = part_id * band_rows
    live_mask = jnp.arange(pattern_len, dtype=jnp.int32)[None, :] < tile_counts[:, None]
    own_live = lax.dynamic_slice_in_dim(
        row_block(live_mask, group_id), part_id * local_tiles, local_tiles
    )
    keep_rows = jnp.repeat(own_live, tile_rows)
    masked_l = jnp.where(keep_rows[:, None], l_offdiag, jnp.zeros_like(l_offdiag))
    piece = lax.all_gather(diag_inverse, "rows", axis=0, tiled=True)
    u_total = jnp.dot(masked_l, piece, preferred_element_type=jnp.float32)
    own_cols = lax.dynamic_slice_in_dim(piece, band_start, band_rows, 1)
    d_total = lax.dot_general(
        own_cols, piece, (((0,), (0,)), ((), ())), preferred_element_type=jnp.float32
    )
    u_total, base_diag = (u_total, d_total)
    u_factor = u_total.astype(jnp.bfloat16)
    owned_tile = jnp.sum(
        jnp.arange(pool_size, dtype=jnp.int32) * (tile_owner == group_id).astype(jnp.int32)
    )
    send_flag = jnp.any((patterns == owned_tile) & live_mask, axis=1)
    own_pattern = row_block(patterns, group_id)
    sources = jnp.take(tile_owner, own_pattern, axis=0)
    col_tiles = lax.dynamic_slice_in_dim(patterns, part_id * local_tiles, local_tiles, 1)
    stored_blocks = anc_store.reshape(tile_rows, pool_size, tile_rows)
    picked = jnp.take(stored_blocks, col_tiles, axis=1)
    picked = jnp.transpose(picked, (1, 0, 2, 3)).reshape(
        group_count, tile_rows, local_tiles * tile_rows
    )
    outgoing = jnp.where(send_flag[:, None, None], picked, jnp.zeros_like(picked))
    incoming = lax.all_to_all(outgoing, "snode", split_axis=0, concat_axis=0, tiled=True)
    arranged = jnp.take(incoming, sources, axis=0).reshape(
        pattern_len * tile_rows, local_tiles * tile_rows
    )
    own_rows = lax.all_to_all(arranged, "rows", split_axis=0, concat_axis=1, tiled=True)
    y_block = jnp.dot(
        own_rows,
        lax.all_gather(u_factor, "rows", axis=0, tiled=True),
        preferred_element_type=jnp.float32,
    )
    offdiag = (-y_block).astype(jnp.bfloat16)
    partial_diag = lax.dot_general(
        u_factor, offdiag, (((0,), (0,)), ((), ())), preferred_element_type=jnp.float32
    )
    whole_update = lax.psum(partial_diag.astype(jnp.bfloat16), "rows").astype(jnp.float32)
    reduced = lax.dynamic_slice_in_dim(whole_update, band_start, band_rows, 0)
    return (offdiag, base_diag - reduced)


def solution(mesh):
    in_specs = (
        P("snode", None),
        P(),
        P(),
        P(),
        P(("snode", "rows"), None),
        P(("snode", "rows"), None),
    )
    out_specs = (P(("snode", "rows"), None), P(("snode", "rows"), None))
    return jax.shard_map(
        per_device, mesh=mesh, in_specs=in_specs, out_specs=out_specs, check_vma=False
    )
```

profile of v0, /device:TPU:8, one launch (start us, length us, event | category | flops | bytes accessed | tf_op | source)
XLA Modules:
  0.0 179.3 jit_solution(5158815995826037886)
XLA Ops:
  7.2 0.7 and_bitcast_fusion
  7.9 3.2 %copy.8 = bf16[128,8192]{0,1:T(8,128)(2,1)S(1)} copy(bf16[128,8192]{1,0:T(8,128)(2,1)} %param.6) | data formatting | bytes 4194304 | tf_op args[0]
  11.1 2.9 %copy.9 = bf16[128,64,128]{2,0,1:T(8,128)(2,1)} copy(bf16[128,64,128]{0,2,1:T(8,128)(2,1)S(1)} %bitcast.37) | data formatting | bytes 4194304 | tf_op jit(solution)/shard_map/reshape | solution.py:42
  14.0 2.6 %gather_fusion.1 = bf16[64,128,128]{2,1,0:T(8,128)(2,1)S(1)} fusion(bf16[128,64,128]{2,0,1:T(8,128)(2,1)} %copy.9, s32[1024]{0:T(1024)S(1)} %pad_clamp_fusion.1), kind=kCustom, calls=%fused_computation.1 | custom fusion | bytes 4194560 | tf_op jit(solution)/shard_map/jit(_take)/gather | solution.py:43
  16.6 0.0 copy-done
  16.6 0.6 fusion.6
  17.2 0.0 copy-done.6
  17.3 0.7 iota_compare_fusion
  17.9 1.7 bitcast_select_fusion
  19.6 16.7 %all-to-all-start = ((bf16[64,128,128]{2,1,0:T(8,128)(2,1)}), bf16[64,128,128]{2,1,0:T(8,128)(2,1)S(1)}, u32[]{:S(2)}, u32[]{:S(2)}) async-start(bf16[64,128,128]{2,1,0:T(8,128)(2,1)} %bitcast_select_fusion), calls=%async_computation | async-start | bytes 4194304 | tf_op jit(solution)/shard_map/all_to_all | solution.py:48
  36.3 0.0 all-gather.2.cloned.1.call-start
  36.4 0.6 dynamic_slice.22
  37.0 0.0 copy-done.4
  37.0 13.4 %all_gather.6 = bf16[512,512]{1,0:T(8,128)(2,1)S(1)} all-gather(bf16[64,512]{1,0:T(8,128)(2,1)S(1)} %copy-done.4), channel_id=1, replica_groups=mesh['snode'=64,'rows'=8] {'rows'}, dimensions={0}, use_global_device_ids=true | all-gather | bytes 589824 | tf_op jit(solution)/shard_map/all_gather | solution.py:27
  50.4 1.5 convolution_convert_fusion.1
  52.0 0.0 all-gather.2.cloned.1.call-update
  52.0 0.0 all-reduce.2.cloned.1.call-start
  52.0 0.2 dynamic-slice_reduce_fusion
  52.2 0.6 gather_fusion
  52.9 36.3 %all-to-all-done = bf16[64,128,128]{2,1,0:T(8,128)(2,1)S(1)} async-done(((bf16[64,128,128]{2,1,0:T(8,128)(2,1)}), bf16[64,128,128]{2,1,0:T(8,128)(2,1)S(1)}, u32[]{:S(2)}, u32[]{:S(2)}) %all-to-all-start) | async-done | bytes 2097184 | tf_op jit(solution)/shard_map/all_to_all | solution.py:48
  89.2 0.6 gather_fusion.2
  89.8 0.1 broadcast_select_fusion
  89.9 11.6 %all_to_all.21 = bf16[8,128,128]{2,1,0:T(8,128)(2,1)S(1)} all-to-all(bf16[8,128,128]{2,1,0:T(8,128)(2,1)S(1)} %broadcast_select_fusion), channel_id=1, replica_groups=mesh['snode'=64,'rows'=8] {'rows'}, dimensions={0} | all-to-all | bytes 524288 | tf_op jit(solution)/shard_map/all_to_all | solution.py:52
  101.6 0.2 copy.10
  101.8 0.0 all-gather.2.cloned.1.call-done
  101.8 1.6 fusion
  103.3 0.0 copy-done.1
  103.4 0.0 copy-start.2
  103.4 1.1 convolution_convert_fusion
  104.5 0.0 all-reduce.2.cloned.1.call-update
  104.5 66.2 %all-reduce.2.cloned.1.call-done = bf16[512,512]{1,0:T(8,128)(2,1)} async-done(((bf16[512,512]{1,0:T(8,128)(2,1)}), bf16[512,512]{1,0:T(8,128)(2,1)}) %all-reduce.2.cloned.1.call-update) | async-done | bytes 524304 | tf_op jit(solution)/shard_map/psum | solution.py:62
  170.7 1.8 %convolution_subtract_fusion = f32[64,512]{1,0:T(8,128)} fusion(bf16[512,512]{1,0:T(8,128)(2,1)S(1)} %all_gather.6, s32[]{:T(128)S(6)} %select_n.116, bf16[512,512]{1,0:T(8,128)(2,1)} %all-reduce.2.cloned.1.call-done), kind=kOutput, calls=%fused_computation.9 | convolution fusion | flops 33619968 | bytes 852992 | tf_op jit(solution)/shard_map/dot_general | solution.py:30
  (15 shorter events, 0.1 us)
Async XLA Ops:
  14.0 2.6 %copy-start = (s32[64]{0:T(128)S(1)}, s32[64]{0:T(128)}, u32[]{:S(2)}) copy-start(s32[64]{0:T(128)} %param.9) | copy-start | bytes 772
  14.0 3.2 %copy-start.5 = (s32[64,8]{0,1:T(8,128)S(1)}, s32[64,8]{0,1:T(8,128)}, u32[]{:S(2)}) copy-start(s32[64,8]{0,1:T(8,128)} %param.7) | copy-start | bytes 6148
  14.0 3.2 %copy-start.6 = (s32[64]{0:T(128)S(1)}, s32[64]{0:T(128)}, u32[]{:S(2)}) copy-start(s32[64]{0:T(128)} %param.8) | copy-start | bytes 772
  19.6 17.4 %copy-start.4 = (bf16[64,512]{1,0:T(8,128)(2,1)S(1)}, bf16[64,512]{1,0:T(8,128)(2,1)}, u32[]{:S(2)}) copy-start(bf16[64,512]{1,0:T(8,128)(2,1)} %param.11) | copy-start | bytes 196612
  19.6 30.8 %copy-start.3 = (bf16[128,512]{1,0:T(8,128)(2,1)S(1)}, bf16[128,512]{1,0:T(8,128)(2,1)}, u32[]{:S(2)}) copy-start(bf16[128,512]{1,0:T(8,128)(2,1)} %param.10) | copy-start | bytes 393220
  19.6 69.6 %all-to-all-start = ((bf16[64,128,128]{2,1,0:T(8,128)(2,1)}), bf16[64,128,128]{2,1,0:T(8,128)(2,1)S(1)}, u32[]{:S(2)}, u32[]{:S(2)}) async-start(bf16[64,128,128]{2,1,0:T(8,128)(2,1)} %bitcast_select_fusion), calls=%async_computation | async-start | bytes 4194304 | tf_op jit(solution)/shard_map/all_to_all | solution.py:48
  36.3 65.5 %all-gather.2.cloned.1.call-start = ((), (), s32[]{:S(2)}) async-start(), calls=%async_computation.2 | async-start | bytes 1179648 | tf_op jit(solution)/shard_map/all_gather | solution.py:55
  52.0 51.4 %copy-start.1 = (bf16[128,512]{1,0:T(8,128)(2,1)S(1)}, bf16[128,512]{1,0:T(8,128)(2,1)}, u32[]{:S(2)}) copy-start(bf16[128,512]{1,0:T(8,128)(2,1)} %convolution_convert_fusion.1) | copy-start | bytes 393220
  52.0 118.7 %all-reduce.2.cloned.1.call-start = ((), (), s32[]{:S(2)}) async-start(), calls=%async_computation.3 | async-start | bytes 1048576 | tf_op jit(solution)/shard_map/psum | solution.py:62
  103.4 69.1 %copy-start.2 = (bf16[128,512]{1,0:T(8,128)(2,1)}, bf16[128,512]{1,0:T(8,128)(2,1)S(1)}, u32[]{:S(2)}) copy-start(bf16[128,512]{1,0:T(8,128)(2,1)S(1)} %fusion) | copy-start | bytes 393220
Sparse Core Ops, SparseCore 0:
  52.1 28.7 all-gather.1
  104.6 65.9 all-reduce.1
where the time goes:
time: 180 us; the launch traced here: 179 us
  waiting for transfers between devices  103 us (57%)
  blocking collectives  25.1 us (14%)
  starting transfers between devices  16.8 us (9%)
  between operations  14.2 us (8%)
  local copies, waits for them, and re-layouts  10.9 us (6%)
  matrix products  6 us (3%)
  other arithmetic  3.82 us (2%)
    psum x1, waiting for transfers between devices, per_device(): lax.psum(partial_diag.astype(jnp.bfloat16), 'rows').astype(jnp.float32)  66.2 us
    all_to_all x1, waiting for transfers between devices, per_device(): lax.all_to_all(outgoing, 'snode', split_axis=0, concat_axis=0, tiled=True)  36.3 us
    all_to_all x1, starting transfers between devices, per_device(): lax.all_to_all(outgoing, 'snode', split_axis=0, concat_axis=0, tiled=True)  16.7 us
    all_gather x1, blocking collectives, per_device(): piece = lax.all_gather(diag_inverse, 'rows', axis=0, tiled=True)  13.4 us
    all_to_all x1, blocking collectives, per_device(): lax.all_to_all(arranged, 'rows', split_axis=0, concat_axis=1, tiled=True)  11.6 us
  transfers between devices with their start and end apart: 3, of which 2 were waited for; matrix products, arithmetic and copies ran while one was open for 2% of the time, Pallas kernels for 0%

commit v1 on v0

--- a/solution.py
+++ b/solution.py
@@ -2,6 +2,7 @@
 import jax.numpy as jnp
 from jax import lax
 from jax.sharding import PartitionSpec as P
+from jax.lax import all_to_all, axis_size
 
 
 def row_block(matrix, index):
@@ -24,7 +25,15 @@
     )
     keep_rows = jnp.repeat(own_live, tile_rows)
     masked_l = jnp.where(keep_rows[:, None], l_offdiag, jnp.zeros_like(l_offdiag))
-    piece = lax.all_gather(diag_inverse, "rows", axis=0, tiled=True)
+    piece = jnp.concatenate(
+        all_to_all(
+            jnp.stack([diag_inverse for _ in range(axis_size("rows"))], axis=0),
+            "rows",
+            split_axis=0,
+            concat_axis=0,
+        ),
+        axis=0,
+    )
     u_total = jnp.dot(masked_l, piece, preferred_element_type=jnp.float32)
     own_cols = lax.dynamic_slice_in_dim(piece, band_start, band_rows, 1)
     d_total = lax.dot_general(

time: 180 us -> 188 us (1.044)
  waiting for transfers between devices: 103 us -> 118 us
  blocking collectives: 25.1 us -> 11.3 us
  starting transfers between devices: 16.8 us -> 21.1 us
    all_to_all x1, waiting for transfers between devices: 36.3 us -> 50.3 us  [per_device(): lax.all_to_all(outgoing, 'snode', split_axis=0, concat_axis=0, tiled=True)]
    all_gather x1 -> x0, blocking collectives: 13.4 us -> none  [per_device(): piece = lax.all_gather(diag_inverse, 'rows', axis=0, tiled=True)]
    all_to_all x0 -> x1, starting transfers between devices: none -> 4.3 us  [per_device(): all_to_all(jnp.stack([diag_inverse for _ in range(axis_size('rows'))], ax...]
  transfers between devices with their start and end apart: 3 -> 4, of which waited for: 2 -> 2; matrix products, arithmetic and copies ran while one was open for 2% -> 9% of each run, Pallas kernels for 0% -> 0%
where the time goes in v1:
time: 188 us; the launch traced here: 187 us
  waiting for transfers between devices  118 us (63%)
  starting transfers between devices  21.1 us (11%)
  between operations  14.2 us (8%)
  local copies, waits for them, and re-layouts  12.6 us (7%)
  blocking collectives  11.3 us (6%)
  matrix products  6.01 us (3%)
  other arithmetic  3.82 us (2%)
    psum x1, waiting for transfers between devices, per_device(): lax.psum(partial_diag.astype(jnp.bfloat16), 'rows').astype(jnp.float32)  68 us
    all_to_all x1, waiting for transfers between devices, per_device(): lax.all_to_all(outgoing, 'snode', split_axis=0, concat_axis=0, tiled=True)  50.3 us
    all_to_all x1, starting transfers between devices, per_device(): lax.all_to_all(outgoing, 'snode', split_axis=0, concat_axis=0, tiled=True)  16.7 us
    all_to_all x1, blocking collectives, per_device(): lax.all_to_all(arranged, 'rows', split_axis=0, concat_axis=1, tiled=True)  11.3 us
    all_to_all x1, starting transfers between devices, per_device(): all_to_all(jnp.stack([diag_inverse for _ in range(axis_size('rows'))], ax...  4.3 us
  transfers between devices with their start and end apart: 4, of which 2 were waited for; matrix products, arithmetic and copies ran while one was open for 9% of the time, Pallas kernels for 0%

profile of v1, /device:TPU:8, one launch (start us, length us, event | category | flops | bytes accessed | tf_op | source)
XLA Modules:
  0.0 187.5 jit_solution(7721786729033643407)
XLA Ops:
  7.2 1.7 stack.2
  8.8 4.3 %all-to-all-start.2 = ((bf16[8,64,512]{2,1,0:T(8,128)(2,1)}), bf16[8,64,512]{2,1,0:T(8,128)(2,1)S(1)}, u32[]{:S(2)}, u32[]{:S(2)}) async-start(bf16[8,64,512]{2,1,0:T(8,128)(2,1)} %stack.2), calls=%async_computation.2 | async-start | bytes 1048576 | tf_op jit(solution)/shard_map/all_to_all | solution.py:29
  13.2 0.7 and_bitcast_fusion
  13.9 3.2 %copy.8 = bf16[128,8192]{0,1:T(8,128)(2,1)S(1)} copy(bf16[128,8192]{1,0:T(8,128)(2,1)} %param.6) | data formatting | bytes 4194304 | tf_op args[0]
  17.1 2.9 %copy.9 = bf16[128,64,128]{2,0,1:T(8,128)(2,1)} copy(bf16[128,64,128]{0,2,1:T(8,128)(2,1)S(1)} %bitcast.38) | data formatting | bytes 4194304 | tf_op jit(solution)/shard_map/reshape | solution.py:51
  20.0 2.6 %gather_fusion.1 = bf16[64,128,128]{2,1,0:T(8,128)(2,1)S(1)} fusion(bf16[128,64,128]{2,0,1:T(8,128)(2,1)} %copy.9, s32[1024]{0:T(1024)S(1)} %pad_clamp_fusion.1), kind=kCustom, calls=%fused_computation.1 | custom fusion | bytes 4194560 | tf_op jit(solution)/shard_map/jit(_take)/gather | solution.py:52
  22.6 0.0 copy-done
  22.6 0.6 fusion.6
  23.3 0.7 iota_compare_fusion
  23.9 1.7 bitcast_select_fusion
  25.6 0.0 all-to-all-done.2
  25.6 16.7 %all-to-all-start = ((bf16[64,128,128]{2,1,0:T(8,128)(2,1)}), bf16[64,128,128]{2,1,0:T(8,128)(2,1)S(1)}, u32[]{:S(2)}, u32[]{:S(2)}) async-start(bf16[64,128,128]{2,1,0:T(8,128)(2,1)} %bitcast_select_fusion), calls=%async_computation | async-start | bytes 4194304 | tf_op jit(solution)/shard_map/all_to_all | solution.py:57
  42.3 0.0 all-gather.2.cloned.1.call-start
  42.4 0.6 dynamic_slice.22
  43.0 1.5 convolution_convert_fusion.1
  44.5 0.0 all-gather.2.cloned.1.call-update
  44.6 0.0 all-reduce.2.cloned.1.call-start
  44.6 0.2 dynamic-slice_reduce_fusion
  44.8 0.6 gather_fusion
  45.5 50.3 %all-to-all-done = bf16[64,128,128]{2,1,0:T(8,128)(2,1)S(1)} async-done(((bf16[64,128,128]{2,1,0:T(8,128)(2,1)}), bf16[64,128,128]{2,1,0:T(8,128)(2,1)S(1)}, u32[]{:S(2)}, u32[]{:S(2)}) %all-to-all-start) | async-done | bytes 2097184 | tf_op jit(solution)/shard_map/all_to_all | solution.py:57
  95.8 0.6 gather_fusion.2
  96.4 0.1 broadcast_select_fusion
  96.5 11.3 %all_to_all.26 = bf16[8,128,128]{2,1,0:T(8,128)(2,1)S(1)} all-to-all(bf16[8,128,128]{2,1,0:T(8,128)(2,1)S(1)} %broadcast_select_fusion), channel_id=1, replica_groups=mesh['snode'=64,'rows'=8] {'rows'}, dimensions={0} | all-to-all | bytes 524288 | tf_op jit(solution)/shard_map/all_to_all | solution.py:61
  107.9 0.2 copy.10
  108.1 0.0 all-gather.2.cloned.1.call-done
  108.1 1.6 fusion
  109.7 0.0 copy-start.2
  109.7 1.1 convolution_convert_fusion
  110.8 0.0 all-reduce.2.cloned.1.call-update
  110.8 68.0 %all-reduce.2.cloned.1.call-done = bf16[512,512]{1,0:T(8,128)(2,1)} async-done(((bf16[512,512]{1,0:T(8,128)(2,1)}), bf16[512,512]{1,0:T(8,128)(2,1)}) %all-reduce.2.cloned.1.call-update) | async-done | bytes 524304 | tf_op jit(solution)/shard_map/psum | solution.py:71
  178.8 1.8 convolution_subtract_fusion
  180.6 0.0 copy-done.2
  (15 shorter events, 0.1 us)
Async XLA Ops:
  8.8 16.8 %all-to-all-start.2 = ((bf16[8,64,512]{2,1,0:T(8,128)(2,1)}), bf16[8,64,512]{2,1,0:T(8,128)(2,1)S(1)}, u32[]{:S(2)}, u32[]{:S(2)}) async-start(bf16[8,64,512]{2,1,0:T(8,128)(2,1)} %stack.2), calls=%async_computation.2 | async-start | bytes 1048576 | tf_op jit(solution)/shard_map/all_to_all | solution.py:29
  20.0 2.6 %copy-start = (s32[64]{0:T(128)S(1)}, s32[64]{0:T(128)}, u32[]{:S(2)}) copy-start(s32[64]{0:T(128)} %param.9) | copy-start | bytes 772
  20.0 3.2 %copy-start.4 = (s32[64,8]{0,1:T(8,128)S(1)}, s32[64,8]{0,1:T(8,128)}, u32[]{:S(2)}) copy-start(s32[64,8]{0,1:T(8,128)} %param.7) | copy-start | bytes 6148
  20.0 3.2 %copy-start.5 = (s32[64]{0:T(128)S(1)}, s32[64]{0:T(128)}, u32[]{:S(2)}) copy-start(s32[64]{0:T(128)} %param.8) | copy-start | bytes 772
  25.6 17.4 %copy-start.3 = (bf16[128,512]{1,0:T(8,128)(2,1)S(1)}, bf16[128,512]{1,0:T(8,128)(2,1)}, u32[]{:S(2)}) copy-start(bf16[128,512]{1,0:T(8,128)(2,1)} %param.10) | copy-start | bytes 393220
  25.6 70.2 %all-to-all-start = ((bf16[64,128,128]{2,1,0:T(8,128)(2,1)}), bf16[64,128,128]{2,1,0:T(8,128)(2,1)S(1)}, u32[]{:S(2)}, u32[]{:S(2)}) async-start(bf16[64,128,128]{2,1,0:T(8,128)(2,1)} %bitcast_select_fusion), calls=%async_computation | async-start | bytes 4194304 | tf_op jit(solution)/shard_map/all_to_all | solution.py:57
  42.3 65.7 %all-gather.2.cloned.1.call-start = ((), (), s32[]{:S(2)}) async-start(), calls=%async_computation.3 | async-start | bytes 1179648 | tf_op jit(solution)/shard_map/all_gather | solution.py:64
  44.5 65.1 %copy-start.1 = (bf16[128,512]{1,0:T(8,128)(2,1)S(1)}, bf16[128,512]{1,0:T(8,128)(2,1)}, u32[]{:S(2)}) copy-start(bf16[128,512]{1,0:T(8,128)(2,1)} %convolution_convert_fusion.1) | copy-start | bytes 393220
  44.6 134.3 %all-reduce.2.cloned.1.call-start = ((), (), s32[]{:S(2)}) async-start(), calls=%async_computation.4 | async-start | bytes 1048576 | tf_op jit(solution)/shard_map/psum | solution.py:71
  109.7 71.0 %copy-start.2 = (bf16[128,512]{1,0:T(8,128)(2,1)}, bf16[128,512]{1,0:T(8,128)(2,1)S(1)}, u32[]{:S(2)}) copy-start(bf16[128,512]{1,0:T(8,128)(2,1)S(1)} %fusion) | copy-start | bytes 393220
Sparse Core Ops, SparseCore 0:
  45.9 29.8 all-gather.1
  110.9 67.8 all-reduce.1
